TPU v7x, 256 devices: a whole 4x4x8 slice. The times are simulated.
256 devices in a mesh: paths: 32 (over x, z_lo, core), trades: 8 (over z_hi, y).
Axes of the slice: x: 4, y: 4, z: 8 (z_hi: 2, z_lo: 4; z = z_hi * 4 + z_lo), core: 2. Of those that a mesh axis runs over, the one named last changes fastest.
Arguments:
- basis: bfloat16 [32768, 512], P('paths'), may hold values from -6 to 6
- coef: bfloat16 [512, 16384], P('paths', 'trades'), may hold values from -0.25 to 0.25
- membership: int32 [16384, 512], P('trades'), may hold values from -1 to 1, as said below
- counts: int32 [512], replicated, may hold values from 1 to 63, as said below
- borrow: float32 [512], replicated, may hold values from 0.3 to 3
- lend: float32 [512], replicated, may hold values from 0.3 to 3
Outputs:
- d_basis: float32 [32768, 512], P(('paths', 'trades'))
- d_coef: float32 [512, 16384], P('paths', 'trades')
Inputs may be any that keep to these rules, and one draw needn't show every extreme that they name: Each row of membership has exactly one nonzero entry, 1 or -1, and every set holds at least one trade. counts[s] is the number of nonzero entries in column s of membership; some set holds exactly one trade and some set exactly 63.
All inputs are finite; a program needn't handle non-finite values.
Results may differ from a plain program's by a relative error of at most 0.0042.
Values may be sent and summed in bfloat16 or wider, within the bound.
No kernel may reach another device: no remote copies, remote signals or barrier semaphores. Data moves between devices by JAX's collectives and lax.ppermute only.
A program may use at most 64 MiB of HBM per device.

v0:
```python
import jax
import jax.numpy as jnp
from jax import lax
from jax.sharding import PartitionSpec as P


def funding(netted, scale, borrow, lend):
    scaled = netted * scale
    grad = (borrow * jax.nn.sigmoid(scaled) + lend * jax.nn.sigmoid(-scaled)) * scale
    return grad.astype(jnp.bfloat16)


def body(basis, coef, membership, counts, borrow, lend):
    path_rows = basis.shape[0]
    member = membership.astype(jnp.bfloat16)
    coef_full = lax.all_gather(coef, "paths", axis=0, tiled=True)
    trade_value = jnp.dot(basis, coef_full, preferred_element_type=jnp.float32)
    exposure = jax.nn.softplus(trade_value).astype(jnp.bfloat16)
    partial_net = jnp.dot(exposure, member, preferred_element_type=jnp.float32)
    scale_all = lax.rsqrt(counts.astype(jnp.float32))
    net_share = lax.psum_scatter(partial_net, "trades", scatter_dimension=1, tiled=True)
    width_sets = net_share.shape[1]
    offset_sets = lax.axis_index("trades") * width_sets
    grad_share = funding(
        net_share,
        lax.dynamic_slice_in_dim(scale_all, offset_sets, width_sets, 0),
        lax.dynamic_slice_in_dim(borrow, offset_sets, width_sets, 0),
        lax.dynamic_slice_in_dim(lend, offset_sets, width_sets, 0),
    )
    set_grad = lax.all_gather(grad_share, "trades", axis=1, tiled=True)
    trade_grad = lax.dot_general(
        set_grad, member, (((1,), (1,)), ((), ())), preferred_element_type=jnp.float32
    )
    value_grad = (trade_grad * jax.nn.sigmoid(trade_value)).astype(jnp.bfloat16)
    d_basis = lax.psum_scatter(
        lax.dot_general(
            value_grad, coef_full, (((1,), (1,)), ((), ())), preferred_element_type=jnp.float32
        ),
        "trades",
        scatter_dimension=0,
        tiled=True,
    )
    factor = 1.0 / jnp.sqrt(jnp.float32(path_rows * lax.axis_size("paths")))
    product = lax.dot_general(
        basis, value_grad, (((0,), (0,)), ((), ())), preferred_element_type=jnp.float32
    )
    d_coef = lax.psum_scatter(product * factor, "paths", scatter_dimension=0, tiled=True)
    return (d_basis, d_coef)


def solution(mesh):
    placed = (P("paths", None), P("paths", "trades"), P("trades", None), P(), P(), P())
    return jax.shard_map(
        body,
        mesh=mesh,
        in_specs=placed,
        out_specs=(P(("paths", "trades"), None), P("paths", "trades")),
        check_vma=False,
    )
```

profile of v0, /device:TPU:16, one launch (start us, length us, event | category | flops | bytes accessed | tf_op | source)
XLA Modules:
  0.0 507.9 jit_solution(12075399827394705610)
XLA Ops:
  7.2 0.0 copy-start
  7.2 0.0 all-gather.3.cloned.1.call-start
  7.2 0.7 all-gather.3.cloned.1.call-update
  7.9 0.0 reduce-scatter.6.cloned.1.call-start
  8.0 64.3 %all-gather.3.cloned.1.call-done = bf16[512,2048]{1,0:T(8,128)(2,1)} async-done(((bf16[16,2048]{1,0:T(8,128)(2,1)}), bf16[512,2048]{1,0:T(8,128)(2,1)}) %all-gather.3.cloned.1.call-update) | async-done | bytes 2097168 | tf_op jit(solution)/shard_map/all_gather | solution.py:16
  72.3 0.0 copy-done
  72.3 0.0 copy-start.2
  72.3 4.1 fusion.6
  76.4 0.0 copy-start.4
  76.4 3.2 copy-done.4
  79.6 0.0 copy-done.2
  79.6 0.0 copy-start.1
  79.6 6.7 %fusion.1 = f32[1024,512]{0,1:T(8,128)} fusion(f32[1024,2048]{1,0:T(8,128)S(1)} %fusion.6, s32[2048,512]{1,0:T(8,128)S(1)} %copy-done.2), kind=kOutput, calls=%fused_computation.4 | convolution fusion | flops 2163212288 | bytes 14680064 | tf_op jit(solution)/shard_map/dot_general | solution.py:19
  86.3 0.0 reduce-scatter.6.cloned.1.call-update
  86.3 0.0 all-gather.5.cloned.1.call-start
  86.4 0.8 dynamic_slice.9
  87.1 0.8 dynamic_slice.11
  87.9 0.0 copy-done.1
  87.9 0.1 dynamic_slice.10
  88.0 91.8 %reduce-scatter.6.cloned.1.call-done = f32[1024,64]{0,1:T(8,128)} async-done(((f32[1024,512]{0,1:T(8,128)}), f32[1024,64]{0,1:T(8,128)}) %reduce-scatter.6.cloned.1.call-update) | async-done | bytes 262160 | tf_op jit(solution)/shard_map/reduce_scatter | solution.py:21
  179.7 1.8 multiply_convert_fusion.1
  181.5 0.0 all-gather.5.cloned.1.call-update
  181.6 0.0 copy-start.3
  181.6 0.0 reduce-scatter.8.cloned.1.call-start
  181.6 58.9 %all-gather.5.cloned.1.call-done = bf16[1024,512]{0,1:T(8,128)(2,1)} async-done(((bf16[1024,64]{0,1:T(8,128)(2,1)}), bf16[1024,512]{0,1:T(8,128)(2,1)}) %all-gather.5.cloned.1.call-update) | async-done | bytes 1048592 | tf_op jit(solution)/shard_map/all_gather | solution.py:30
  240.5 8.5 %multiply_convert_fusion = bf16[1024,2048]{1,0:T(8,128)(2,1)S(1)} fusion(f32[1024,2048]{1,0:T(8,128)} %copy-done.4, bf16[1024,512]{0,1:T(8,128)(2,1)} %all-gather.5.cloned.1.call-done, s32[2048,512]{1,0:T(8,128)} %param.8), kind=kOutput, calls=%fused_computation.2 | convolution fusion | flops 2159017984 | bytes 17825792 | tf_op jit(solution)/shard_map/dot_general | solution.py:31
  249.0 0.0 copy-start.5
  249.1 1.9 copy-done.5
  251.0 0.0 copy-done.3
  251.0 3.7 fusion.7
  254.7 0.0 reduce-scatter.8.cloned.1.call-update
  254.8 0.2 reduce-scatter.10.cloned.1.call-start
  255.0 6.5 %multiply_bitcast_fusion = f32[512,2048]{0,1:T(8,128)} fusion(bf16[1024,2048]{1,0:T(8,128)(2,1)} %copy-done.5, bf16[1024,512]{1,0:T(8,128)(2,1)S(1)} %copy-done), kind=kOutput, calls=%fused_computation.3 | convolution fusion | flops 2148532224 | bytes 9437184 | tf_op jit(solution)/shard_map/dot_general | solution.py:44
  261.5 5.4 %copy.10 = f32[512,2048]{1,0:T(8,128)} copy(f32[512,2048]{0,1:T(8,128)} %multiply_bitcast_fusion) | data formatting | bytes 8388608
  266.9 0.0 reduce-scatter.10.cloned.1.call-update
  267.0 79.4 %reduce-scatter.8.cloned.1.call-done = f32[128,512]{1,0:T(8,128)} async-done(((f32[1024,512]{1,0:T(8,128)}), f32[128,512]{1,0:T(8,128)}) %reduce-scatter.8.cloned.1.call-update) | async-done | bytes 262160 | tf_op jit(solution)/shard_map/reduce_scatter | solution.py:35
  346.3 155.0 %reduce-scatter.10.cloned.1.call-done = f32[16,2048]{1,0:T(8,128)} async-done(((f32[512,2048]{1,0:T(8,128)}), f32[16,2048]{1,0:T(8,128)}) %reduce-scatter.10.cloned.1.call-update) | async-done | bytes 131088
  (1 shorter events, 0.0 us)
Async XLA Ops:
  7.2 65.1 %copy-start = (bf16[1024,512]{1,0:T(8,128)(2,1)S(1)}, bf16[1024,512]{1,0:T(8,128)(2,1)}, u32[]{:S(2)}) copy-start(bf16[1024,512]{1,0:T(8,128)(2,1)} %param.6) | copy-start | bytes 3145732
  7.2 65.1 %all-gather.3.cloned.1.call-start = ((), (), s32[]{:S(2)}) async-start(), calls=%async_computation.3 | async-start | bytes 2162688 | tf_op jit(solution)/shard_map/all_gather | solution.py:16
  7.9 171.8 %reduce-scatter.6.cloned.1.call-start = ((), (), s32[]{:S(2)}) async-start(), calls=%async_computation.4 | async-start | bytes 2359296 | tf_op jit(solution)/shard_map/reduce_scatter | solution.py:21
  72.3 7.3 %copy-start.2 = (s32[2048,512]{1,0:T(8,128)S(1)}, s32[2048,512]{1,0:T(8,128)}, u32[]{:S(2)}) copy-start(s32[2048,512]{1,0:T(8,128)} %param.8) | copy-start | bytes 12582916
  76.4 3.2 copy-start.4
  79.6 8.3 %copy-start.1 = (s32[512]{0:T(512)S(1)}, s32[512]{0:T(512)}, u32[]{:S(2)}) copy-start(s32[512]{0:T(512)} %param.9) | copy-start | bytes 6148
  86.3 154.2 %all-gather.5.cloned.1.call-start = ((), (), s32[]{:S(2)}) async-start(), calls=%async_computation.5 | async-start | bytes 1179648 | tf_op jit(solution)/shard_map/all_gather | solution.py:30
  181.6 69.4 %copy-start.3 = (bf16[512,2048]{1,0:T(8,128)(2,1)S(1)}, bf16[512,2048]{1,0:T(8,128)(2,1)}, u32[]{:S(2)}) copy-start(bf16[512,2048]{1,0:T(8,128)(2,1)} %all-gather.3.cloned.1.call-done) | copy-start | bytes 6291460
  181.6 164.8 %reduce-scatter.8.cloned.1.call-start = ((), (), s32[]{:S(2)}) async-start(), calls=%async_computation.6 | async-start | bytes 2359296 | tf_op jit(solution)/shard_map/reduce_scatter | solution.py:35
  249.0 2.0 copy-start.5
  254.8 246.6 %reduce-scatter.10.cloned.1.call-start = ((), (), s32[]{:S(2)}) async-start(), calls=%async_computation.7 | async-start | bytes 4325376
Sparse Core Ops, SparseCore 0:
  9.8 62.4 all-gather.2
  86.4 93.2 reduce-scatter.5
  182.9 57.5 all-gather.4
  254.9 91.4 reduce-scatter.7
  349.3 152.0 reduce-scatter.9
where the time goes:
time: 508 us
  waiting for transfers between devices  450 us (89%)
  matrix products  29.5 us (6%)
  between operations  13.8 us (3%)
  local copies, waits for them, and re-layouts  12.2 us (2%)
    unnamed x6, waiting for transfers between devices  156 us
    reduce_scatter x1, waiting for transfers between devices, body(): lax.psum_scatter(partial_net, 'trades', scatter_dimension=1, tiled=True)  91.8 us
    reduce_scatter x1, waiting for transfers between devices, body(): lax.psum_scatter(lax.dot_general(value_grad, coef_full, (((1,), (1,)), ((...  79.4 us
    all_gather x1, waiting for transfers between devices, body(): coef_full = lax.all_gather(coef, 'paths', axis=0, tiled=True)  64.3 us
    all_gather x1, waiting for transfers between devices, body(): set_grad = lax.all_gather(grad_share, 'trades', axis=1, tiled=True)  58.9 us
    unnamed x13, local copies, waits for them, and re-layouts  10.6 us
  transfers between devices with their start and end apart: 5, of which 5 were waited for; matrix products, arithmetic and copies ran while one was open for 3% of the time, Pallas kernels for 0%

commit v1 on v0

--- a/solution.py
+++ b/solution.py
@@ -27,7 +27,8 @@
         lax.dynamic_slice_in_dim(borrow, offset_sets, width_sets, 0),
         lax.dynamic_slice_in_dim(lend, offset_sets, width_sets, 0),
     )
-    set_grad = lax.all_gather(grad_share, "trades", axis=1, tiled=True)
+    stack = jnp.stack([grad_share] * lax.axis_size("trades"))
+    set_grad = jnp.concatenate(lax.all_to_all(stack, "trades", 0, 0), axis=1)
     trade_grad = lax.dot_general(
         set_grad, member, (((1,), (1,)), ((), ())), preferred_element_type=jnp.float32
     )

time: 508 us -> 479 us (0.943)
  waiting for transfers between devices: 450 us -> 403 us
  blocking collectives: 0 us -> 19.7 us
    all_gather x1 -> x0, waiting for transfers between devices: 58.9 us -> none  [body(): set_grad = lax.all_gather(grad_share, 'trades', axis=1, tiled=True)]
    all_to_all x0 -> x1, blocking collectives: none -> 19.7 us  [body(): set_grad = jnp.concatenate(lax.all_to_all(stack, 'trades', 0, 0), axis=1)]
    reduce_scatter x1, waiting for transfers between devices: 79.4 us -> 91.1 us  [body(): lax.psum_scatter(lax.dot_general(value_grad, coef_full, (((1,), (1,)), ((...]
    unnamed x6 -> x5, waiting for transfers between devices: 156 us -> 156 us
  transfers between devices with their start and end apart: 5 -> 4, of which waited for: 5 -> 4; matrix products, arithmetic and copies ran while one was open for 3% -> 3% of each run, Pallas kernels for 0% -> 0%
where the time goes in v1:
time: 479 us; the launch traced here: 478 us
  waiting for transfers between devices  403 us (84%)
  matrix products  27.8 us (6%)
  blocking collectives  19.7 us (4%)
  between operations  13.8 us (3%)
  local copies, waits for them, and re-layouts  12.3 us (3%)
    unnamed x5, waiting for transfers between devices  156 us
    reduce_scatter x1, waiting for transfers between devices, body(): lax.psum_scatter(partial_net, 'trades', scatter_dimension=1, tiled=True)  91.8 us
    reduce_scatter x1, waiting for transfers between devices, body(): lax.psum_scatter(lax.dot_general(value_grad, coef_full, (((1,), (1,)), ((...  91.1 us
    all_gather x1, waiting for transfers between devices, body(): coef_full = lax.all_gather(coef, 'paths', axis=0, tiled=True)  64.3 us
    all_to_all x1, blocking collectives, body(): set_grad = jnp.concatenate(lax.all_to_all(stack, 'trades', 0, 0), axis=1)  19.7 us
    unnamed x13, local copies, waits for them, and re-layouts  10.6 us
  transfers between devices with their start and end apart: 4, of which 4 were waited for; matrix products, arithmetic and copies ran while one was open for 3% of the time, Pallas kernels for 0%

profile of v1, /device:TPU:16, one launch (start us, length us, event | category | flops | bytes accessed | tf_op | source)
XLA Modules:
  0.0 477.9 jit_solution(3165041459551390574)
XLA Ops:
  7.2 0.0 copy-start
  7.2 0.0 all-gather.2.cloned.1.call-start
  7.2 0.7 all-gather.2.cloned.1.call-update
  7.9 0.0 reduce-scatter.6.cloned.1.call-start
  8.0 64.3 %all-gather.2.cloned.1.call-done = bf16[512,2048]{1,0:T(8,128)(2,1)} async-done(((bf16[16,2048]{1,0:T(8,128)(2,1)}), bf16[512,2048]{1,0:T(8,128)(2,1)}) %all-gather.2.cloned.1.call-update) | async-done | bytes 2097168 | tf_op jit(solution)/shard_map/all_gather | solution.py:16
  72.3 0.0 copy-done
  72.3 0.0 copy-start.2
  72.3 4.1 fusion.6
  76.4 0.0 copy-start.4
  76.4 3.2 copy-done.4
  79.6 0.0 copy-done.2
  79.6 0.0 copy-start.1
  79.6 6.7 %fusion.1 = f32[1024,512]{0,1:T(8,128)} fusion(f32[1024,2048]{1,0:T(8,128)S(1)} %fusion.6, s32[2048,512]{1,0:T(8,128)S(1)} %copy-done.2), kind=kOutput, calls=%fused_computation.4 | convolution fusion | flops 2163212288 | bytes 14680064 | tf_op jit(solution)/shard_map/dot_general | solution.py:19
  86.3 0.0 reduce-scatter.6.cloned.1.call-update
  86.3 0.0 reduce-scatter.8.cloned.1.call-start
  86.3 0.8 dynamic_slice.9
  87.1 0.8 dynamic_slice.11
  87.9 0.0 copy-done.1
  87.9 0.1 dynamic_slice.10
  87.9 91.8 %reduce-scatter.6.cloned.1.call-done = f32[1024,64]{0,1:T(8,128)} async-done(((f32[1024,512]{0,1:T(8,128)}), f32[1024,64]{0,1:T(8,128)}) %reduce-scatter.6.cloned.1.call-update) | async-done | bytes 262160 | tf_op jit(solution)/shard_map/reduce_scatter | solution.py:21
  179.7 1.2 multiply_convert_fusion.1
  180.9 0.1 stack.2
  181.0 19.7 %all_to_all.5 = bf16[8,1024,64]{1,2,0:T(8,128)(2,1)S(1)} all-to-all(bf16[8,1024,64]{1,2,0:T(8,128)(2,1)S(1)} %stack.2), channel_id=1, replica_groups=mesh['paths'=32,'trades'=8] {'trades'}, dimensions={0} | all-to-all | bytes 2097152 | tf_op jit(solution)/shard_map/all_to_all | solution.py:31
  200.7 0.0 copy-start.3
  200.7 6.9 %multiply_convert_fusion = bf16[1024,2048]{1,0:T(8,128)(2,1)S(1)} fusion(f32[1024,2048]{1,0:T(8,128)} %copy-done.4, bf16[1024,512]{0,1:T(8,128)(2,1)S(1)} %bitcast.13, s32[2048,512]{1,0:T(8,128)} %param.8), kind=kOutput, calls=%fused_computation.2 | convolution fusion | flops 2159017984 | bytes 17825792 | tf_op jit(solution)/shard_map/dot_general | solution.py:32
  207.6 0.0 copy-start.5
  207.6 1.9 copy-done.5
  209.5 0.0 copy-done.3
  209.5 3.7 fusion.7
  213.2 0.0 reduce-scatter.8.cloned.1.call-update
  213.3 0.0 reduce-scatter.10.cloned.1.call-start
  213.3 6.5 %multiply_bitcast_fusion = f32[512,2048]{0,1:T(8,128)} fusion(bf16[1024,2048]{1,0:T(8,128)(2,1)} %copy-done.5, bf16[1024,512]{1,0:T(8,128)(2,1)S(1)} %copy-done), kind=kOutput, calls=%fused_computation.3 | convolution fusion | flops 2148532224 | bytes 9437184 | tf_op jit(solution)/shard_map/dot_general | solution.py:45
  219.9 5.5 %copy.12 = f32[512,2048]{1,0:T(8,128)} copy(f32[512,2048]{0,1:T(8,128)} %multiply_bitcast_fusion) | data formatting | bytes 8388608
  225.3 0.0 reduce-scatter.10.cloned.1.call-update
  225.3 91.1 %reduce-scatter.8.cloned.1.call-done = f32[128,512]{1,0:T(8,128)} async-done(((f32[1024,512]{1,0:T(8,128)}), f32[128,512]{1,0:T(8,128)}) %reduce-scatter.8.cloned.1.call-update) | async-done | bytes 262160 | tf_op jit(solution)/shard_map/reduce_scatter | solution.py:36
  316.5 154.9 %reduce-scatter.10.cloned.1.call-done = f32[16,2048]{1,0:T(8,128)} async-done(((f32[512,2048]{1,0:T(8,128)}), f32[16,2048]{1,0:T(8,128)}) %reduce-scatter.10.cloned.1.call-update) | async-done | bytes 131088
  (1 shorter events, 0.0 us)
Async XLA Ops:
  7.2 65.1 %copy-start = (bf16[1024,512]{1,0:T(8,128)(2,1)S(1)}, bf16[1024,512]{1,0:T(8,128)(2,1)}, u32[]{:S(2)}) copy-start(bf16[1024,512]{1,0:T(8,128)(2,1)} %param.6) | copy-start | bytes 3145732
  7.2 65.1 %all-gather.2.cloned.1.call-start = ((), (), s32[]{:S(2)}) async-start(), calls=%async_computation.4 | async-start | bytes 2162688 | tf_op jit(solution)/shard_map/all_gather | solution.py:16
  7.9 171.8 %reduce-scatter.6.cloned.1.call-start = ((), (), s32[]{:S(2)}) async-start(), calls=%async_computation.5 | async-start | bytes 2359296 | tf_op jit(solution)/shard_map/reduce_scatter | solution.py:21
  72.3 7.3 %copy-start.2 = (s32[2048,512]{1,0:T(8,128)S(1)}, s32[2048,512]{1,0:T(8,128)}, u32[]{:S(2)}) copy-start(s32[2048,512]{1,0:T(8,128)} %param.8) | copy-start | bytes 12582916
  76.4 3.2 copy-start.4
  79.6 8.2 %copy-start.1 = (s32[512]{0:T(512)S(1)}, s32[512]{0:T(512)}, u32[]{:S(2)}) copy-start(s32[512]{0:T(512)} %param.9) | copy-start | bytes 6148
  86.3 230.2 %reduce-scatter.8.cloned.1.call-start = ((), (), s32[]{:S(2)}) async-start(), calls=%async_computation.6 | async-start | bytes 2359296 | tf_op jit(solution)/shard_map/reduce_scatter | solution.py:36
  200.7 8.8 %copy-start.3 = (bf16[512,2048]{1,0:T(8,128)(2,1)S(1)}, bf16[512,2048]{1,0:T(8,128)(2,1)}, u32[]{:S(2)}) copy-start(bf16[512,2048]{1,0:T(8,128)(2,1)} %all-gather.2.cloned.1.call-done) | copy-start | bytes 6291460
  207.6 1.9 copy-start.5
  213.3 258.1 %reduce-scatter.10.cloned.1.call-start = ((), (), s32[]{:S(2)}) async-start(), calls=%async_computation.7 | async-start | bytes 4325376
Sparse Core Ops, SparseCore 0:
  9.8 62.4 all-gather.1
  86.4 93.2 reduce-scatter.5
  213.4 103.0 reduce-scatter.7
  319.4 151.8 reduce-scatter.9
